TPU v7x, 512 devices: a whole 4x8x8 slice. The times are simulated.
512 devices in a mesh: gx: 32 (over z_hi, y, core), gz: 16 (over z_lo, x).
Axes of the slice: x: 4, y: 8, z: 8 (z_hi: 2, z_lo: 4; z = z_hi * 4 + z_lo), core: 2. Of those that a mesh axis runs over, the one named last changes fastest.
Arguments:
- velocity: float32 [3, 2, 6144, 4096], P(None, None, 'gz', 'gx'), may hold values from -6 to 6
- metric_index: int32 [4096], P('gx'), may hold values from 0 to 63
- jac_table: float32 [64], replicated, may hold values from 0.5 to 2
- bend_table: float32 [64], replicated, may hold values from -1 to 1
Outputs:
- first_derivative: float32 [3, 2, 6144, 4096], P(None, None, 'gz', 'gx')
- second_derivative: float32 [3, 2, 6144, 4096], P(None, None, 'gz', 'gx')
- plane_energy: float32 [3, 2], replicated
Inputs may be any that keep to these rules, and one draw needn't show every extreme that they name: `metric_index`: each entry names a row of the metric tables.
All inputs are finite; a program needn't handle non-finite values.
Results may differ from a plain program's by a relative error of at most 0.00007.
Values sent between devices are 32-bit elements; how exact they have to be, the bound alone decides.
A program may use at most 64 MiB of HBM per device.

v0:
```python
import math
import jax
import jax.numpy as jnp
from jax import lax
from jax.sharding import PartitionSpec as P

alpha_one = 1.0 / 3.0
alpha_two = 2.0 / 11.0
reach = 24
highest = lax.Precision.HIGHEST


def band_matrix(rows, alpha):
    root = math.sqrt(1.0 - 4.0 * alpha * alpha)
    ratio = (1.0 - root) / (2.0 * alpha)
    factor = ratio / alpha / (1.0 - ratio * ratio)
    row_ids = jnp.arange(rows, dtype=jnp.int32)[:, None]
    col_ids = jnp.arange(rows + 2 * reach, dtype=jnp.int32)[None, :]
    offset = jnp.abs(col_ids - reach - row_ids)
    parity = jnp.where(offset % 2 == 0, 1.0, -1.0)
    power = jnp.exp(offset.astype(jnp.float32) * math.log(ratio))
    return jnp.where(offset <= reach, factor * parity * power, 0.0)


def stencil_matrix(rows, weights):
    row_ids = jnp.arange(rows, dtype=jnp.int32)[:, None]
    col_ids = jnp.arange(rows + 4, dtype=jnp.int32)[None, :]
    shift_ids = col_ids - row_ids - 2
    total = jnp.zeros((rows, rows + 4), jnp.float32)
    for shift_k, weight in zip((-2, -1, 0, 1, 2), weights):
        total = total + jnp.where(shift_ids == shift_k, weight, 0.0)
    return total


def line_operator(alpha, weights):
    block = 128
    band = band_matrix(block, alpha)
    stencil = stencil_matrix(block + 2 * reach, weights)
    joined = jnp.dot(band, stencil, precision=highest)
    start = block - reach - 2
    return jnp.pad(joined, ((0, 0), (start, 3 * block - start - joined.shape[1])))


def periodic_lines(columns):
    block = 128
    length = columns.shape[-1]
    lead = columns.shape[:-1]
    main = columns.reshape(lead + (length // block, block))
    before = jnp.roll(main, 1, axis=-2)
    after = jnp.roll(main, -1, axis=-2)
    weights_one = (-1.0 / 36.0, -7.0 / 9.0, 0.0, 7.0 / 9.0, 1.0 / 36.0)
    weights_two = (3.0 / 44.0, 12.0 / 11.0, -102.0 / 44.0, 12.0 / 11.0, 3.0 / 44.0)
    results = []
    for alpha, weights in ((alpha_one, weights_one), (alpha_two, weights_two)):
        whole_op = line_operator(alpha, weights)
        part = jnp.einsum("abcnm,im->abcni", before, whole_op[:, :block], precision=highest)
        part = part + jnp.einsum(
            "abcnm,im->abcni", main, whole_op[:, block : 2 * block], precision=highest
        )
        part = part + jnp.einsum(
            "abcnm,im->abcni", after, whole_op[:, 2 * block :], precision=highest
        )
        results.append(part.reshape(lead + (length,)))
    return (results[0], results[1])


def on_device(velocity, metric_index, jac_table, bend_table):
    first_line, second_line = periodic_lines(
        lax.all_to_all(velocity, "gx", split_axis=2, concat_axis=3, tiled=True)
    )
    first_xi = lax.all_to_all(first_line, "gx", split_axis=3, concat_axis=2, tiled=True)
    second_xi = lax.all_to_all(second_line, "gx", split_axis=3, concat_axis=2, tiled=True)
    table_rows = jac_table.shape[0]
    onehot = (metric_index[:, None] == jnp.arange(table_rows, dtype=jnp.int32)[None, :]).astype(
        jnp.float32
    )
    jac = jnp.dot(onehot, jac_table, precision=highest)
    bend = jnp.dot(onehot, bend_table, precision=highest)
    first = first_xi / jac
    second = (second_xi - bend * first) / (jac * jac)
    total_points = (
        metric_index.shape[0] * lax.axis_size("gx") * velocity.shape[2] * lax.axis_size("gz")
    )
    sums = lax.psum(jnp.sum(first * first, axis=(2, 3)), ("gx", "gz"))
    return (first, second, sums / total_points)


def solution(mesh):
    in_specs = (P(None, None, "gz", "gx"), P("gx"), P(), P())
    out_specs = (P(None, None, "gz", "gx"), P(None, None, "gz", "gx"), P())
    return jax.shard_map(
        on_device, mesh=mesh, in_specs=in_specs, out_specs=out_specs, check_vma=False
    )
```

profile of v0, /device:TPU:1, one launch (start us, length us, event | category | flops | bytes accessed | tf_op | source)
XLA Modules:
  0.0 331.4 jit_solution(7821478155496641981)
XLA Ops:
  0.6 3.2 copy.49
  3.9 17.2 %all-to-all-start = ((f32[3,2,384,128]{3,0,1,2:T(4,128)}), f32[3,2,384,128]{3,0,1,2:T(4,128)S(1)}, u32[]{:S(2)}, u32[]{:S(2)}) async-start(f32[3,2,384,128]{3,0,1,2:T(4,128)} %copy.49), calls=%async_computation | async-start | bytes 3145728 | tf_op jit(solution)/shard_map/all_to_all | solution.py:69
  21.1 1.1 fusion.18
  22.2 41.3 %all-to-all-done = f32[3,2,384,128]{3,0,1,2:T(4,128)S(1)} async-done(((f32[3,2,384,128]{3,0,1,2:T(4,128)}), f32[3,2,384,128]{3,0,1,2:T(4,128)S(1)}, u32[]{:S(2)}, u32[]{:S(2)}) %all-to-all-start) | async-done | bytes 1179680 | tf_op jit(solution)/shard_map/all_to_all | solution.py:69
  65.2 1.1 fusion.7
  67.4 2.2 fusion.1
  69.6 11.0 %copy.89 = f32[3,2,12,32,128]{2,1,0,4,3:T(2,128)} copy(f32[3,2,12,32,128]{4,3,2,1,0:T(8,128)} %fusion.1) | data formatting | bytes 2359296 | tf_op jit(solution)/shard_map/reshape | solution.py:63
  80.6 19.5 %reshape.37 = f32[32,1,9216]{2,1,0:T(1,128)} reshape(f32[4096,3,2,12]{3,2,1,0:T(2,128)} %bitcast.61) | data formatting | bytes 2359296
  100.1 6.5 %all-to-all-start.1 = ((f32[32,1,9216]{2,1,0:T(1,128)}), f32[32,1,9216]{2,1,0:T(1,128)}, u32[]{:S(2)}, u32[]{:S(2)}) async-start(f32[32,1,9216]{2,1,0:T(1,128)} %reshape.37), calls=%async_computation.1 | async-start | bytes 2359296 | tf_op jit(solution)/shard_map/all_to_all | solution.py:71
  107.4 1.1 fusion.6
  108.5 1.1 fusion.4
  109.6 1.1 fusion.3
  110.7 9.0 %copy.90 = f32[3,2,12,32,128]{2,1,0,4,3:T(2,128)} copy(f32[3,2,12,32,128]{4,3,2,1,0:T(8,128)S(1)} %fusion.3) | data formatting | bytes 2359296 | tf_op jit(solution)/shard_map/reshape | solution.py:63
  119.8 19.5 %reshape.39 = f32[32,1,9216]{2,1,0:T(1,128)} reshape(f32[4096,3,2,12]{3,2,1,0:T(2,128)} %bitcast.62) | data formatting | bytes 2359296
  140.0 11.7 %all-to-all-start.2 = ((f32[32,1,9216]{2,1,0:T(1,128)}), f32[32,1,9216]{2,1,0:T(1,128)S(1)}, u32[]{:S(2)}, u32[]{:S(2)}) async-start(f32[32,1,9216]{2,1,0:T(1,128)} %reshape.39), calls=%async_computation.2 | async-start | bytes 2359296 | tf_op jit(solution)/shard_map/all_to_all | solution.py:72
  152.4 4.8 %reduce.2 = f32[32,9216]{1,0:T(8,128)S(1)} reduce(f32[32,1,9216]{2,1,0:T(1,128)} %all-to-all-done.1, f32[]{:T(128)} %broadcast.111), dimensions={1}, to_apply=%all_to_all.40.reduce_sub_computation | reduce | bytes 2359300 | tf_op jit(solution)/shard_map/all_to_all | solution.py:71
  157.2 21.8 %reshape.38 = f32[4096,3,2,12]{3,2,1,0:T(2,128)} reshape(f32[32,9216]{1,0:T(8,128)S(1)} %reduce.2) | data formatting | bytes 2359296
  179.1 10.2 %copy.82 = f32[3,2,12,32,128]{4,3,1,2,0:T(8,128)S(1)} copy(f32[3,2,12,32,128]{2,1,0,4,3:T(2,128)} %bitcast.63) | data formatting | bytes 2359296 | tf_op jit(solution)/shard_map/all_to_all | solution.py:71
  190.1 100.3 %psum.7 = f32[3,2]{1,0:T(4,128)S(1)} all-reduce(f32[3,2]{1,0:T(4,128)S(1)} %multiply_reduce_fusion), channel_id=1, replica_groups=mesh['gx'=32,'gz'=16] {'gx','gz'}, use_global_device_ids=true, to_apply=%region_1.2 | all-reduce | flops 6 | bytes 48 | tf_op jit(solution)/shard_map/psum | solution.py:84
  291.9 3.5 %reduce.1 = f32[32,9216]{1,0:T(8,128)S(1)} reduce(f32[32,1,9216]{2,1,0:T(1,128)S(1)} %all-to-all-done.2, f32[]{:T(128)} %broadcast.111), dimensions={1}, to_apply=%all_to_all.44.reduce_sub_computation | reduce | bytes 2359300 | tf_op jit(solution)/shard_map/all_to_all | solution.py:72
  295.5 21.8 %reshape.40 = f32[4096,3,2,12]{3,2,1,0:T(2,128)} reshape(f32[32,9216]{1,0:T(8,128)S(1)} %reduce.1) | data formatting | bytes 2359296
  317.3 10.2 %copy.88 = f32[3,2,12,32,128]{4,3,1,2,0:T(8,128)S(1)} copy(f32[3,2,12,32,128]{2,1,0,4,3:T(2,128)} %bitcast.64) | data formatting | bytes 2359296 | tf_op jit(solution)/shard_map/all_to_all | solution.py:72
  329.2 1.1 copy.67
  330.3 1.1 copy.66
  (35 shorter events, 9.1 us)
Async XLA Ops:
  0.6 151.0 %copy-start = (f32[64]{0:T(128)S(1)}, f32[64]{0:T(128)}, u32[]{:S(2)}) copy-start(f32[64]{0:T(128)} %param.6) | copy-start | bytes 772
  3.9 59.7 %all-to-all-start = ((f32[3,2,384,128]{3,0,1,2:T(4,128)}), f32[3,2,384,128]{3,0,1,2:T(4,128)S(1)}, u32[]{:S(2)}, u32[]{:S(2)}) async-start(f32[3,2,384,128]{3,0,1,2:T(4,128)} %copy.49), calls=%async_computation | async-start | bytes 3145728 | tf_op jit(solution)/shard_map/all_to_all | solution.py:69
  64.3 0.6 copy-start.5
  64.3 2.0 copy-start.3
  64.3 0.9 copy-start.2
  100.1 39.8 %all-to-all-start.1 = ((f32[32,1,9216]{2,1,0:T(1,128)}), f32[32,1,9216]{2,1,0:T(1,128)}, u32[]{:S(2)}, u32[]{:S(2)}) async-start(f32[32,1,9216]{2,1,0:T(1,128)} %reshape.37), calls=%async_computation.1 | async-start | bytes 2359296 | tf_op jit(solution)/shard_map/all_to_all | solution.py:71
  106.6 0.8 copy-start.6
  107.4 1.1 copy-start.4
  139.3 12.4 %copy-start.7 = (s32[128]{0:T(128)S(1)}, s32[128]{0:T(128)}, u32[]{:S(2)}) copy-start(s32[128]{0:T(128)} %param.5) | copy-start | bytes 1540
  140.0 152.0 %all-to-all-start.2 = ((f32[32,1,9216]{2,1,0:T(1,128)}), f32[32,1,9216]{2,1,0:T(1,128)S(1)}, u32[]{:S(2)}, u32[]{:S(2)}) async-start(f32[32,1,9216]{2,1,0:T(1,128)} %reshape.39), calls=%async_computation.2 | async-start | bytes 2359296 | tf_op jit(solution)/shard_map/all_to_all | solution.py:72
  189.2 0.7 copy-start.8
  330.3 1.1 copy-start.1
where the time goes:
time: 333 us; the launch traced here: 331 us
  local copies, waits for them, and re-layouts  134 us (40%)
  blocking collectives  100 us (30%)
  waiting for transfers between devices  42 us (13%)
  starting transfers between devices  35.3 us (11%)
  matrix products  9.68 us (3%)
  other arithmetic  9.4 us (3%)
    psum x1, blocking collectives, on_device(): sums = lax.psum(jnp.sum(first * first, axis=(2, 3)), ('gx', 'gz'))  100 us
    unnamed x26, local copies, waits for them, and re-layouts  90.1 us
    all_to_all x1, waiting for transfers between devices, on_device(): lax.all_to_all(velocity, 'gx', split_axis=2, concat_axis=3, tiled=True)  41.3 us
    reshape x2, local copies, waits for them, and re-layouts, periodic_lines(): results.append(part.reshape(lead + (length,)))  20 us
    all_to_all x1, starting transfers between devices, on_device(): lax.all_to_all(velocity, 'gx', split_axis=2, concat_axis=3, tiled=True)  17.2 us
    all_to_all x1, starting transfers between devices, on_device(): lax.all_to_all(second_line, 'gx', split_axis=3, concat_axis=2, tiled=True)  11.7 us
    all_to_all x3, local copies, waits for them, and re-layouts, on_device(): lax.all_to_all(second_line, 'gx', split_axis=3, concat_axis=2, tiled=True)  11.6 us
    all_to_all x2, local copies, waits for them, and re-layouts, on_device(): lax.all_to_all(first_line, 'gx', split_axis=3, concat_axis=2, tiled=True)  11.1 us
  transfers between devices with their start and end apart: 3, of which 2 were waited for; matrix products, arithmetic and copies ran while one was open for 22% of the time, Pallas kernels for 0%

commit v1 on v0

--- a/solution.py
+++ b/solution.py
@@ -8,6 +8,10 @@
 alpha_two = 2.0 / 11.0
 reach = 24
 highest = lax.Precision.HIGHEST
+
+
+def enter_table(local_values):
+    return lax.all_gather(local_values, ("gx", "gz")).sum(axis=0)
 
 
 def band_matrix(rows, alpha):
@@ -81,7 +85,7 @@
     total_points = (
         metric_index.shape[0] * lax.axis_size("gx") * velocity.shape[2] * lax.axis_size("gz")
     )
-    sums = lax.psum(jnp.sum(first * first, axis=(2, 3)), ("gx", "gz"))
+    sums = enter_table(jnp.sum(first * first, axis=(2, 3)))
     return (first, second, sums / total_points)
 
 

time: 333 us -> 1560 us (4.68)
  the two profiles are of different devices: /device:TPU:1 before, /device:TPU:32 now
where the time goes in v1:
time: 1560 us; the launch traced here: 1550 us
  blocking collectives  1320 us (85%)
  local copies, waits for them, and re-layouts  133 us (9%)
  waiting for transfers between devices  38.9 us (2%)
  starting transfers between devices  38 us (2%)
    all_gather x1, blocking collectives, enter_table(): return lax.all_gather(local_values, ('gx', 'gz')).sum(axis=0)  1320 us
    unnamed x27, local copies, waits for them, and re-layouts  89 us
    all_to_all x1, waiting for transfers between devices, on_device(): lax.all_to_all(velocity, 'gx', split_axis=2, concat_axis=3, tiled=True)  38.9 us
  transfers between devices with their start and end apart: 3, of which 1 were waited for; matrix products, arithmetic and copies ran while one was open for 5% of the time, Pallas kernels for 0%

profile of v1, /device:TPU:32, one launch (start us, length us, event | category | flops | bytes accessed | tf_op | source)
XLA Modules:
  0.0 1551.0 jit_solution(6842137458442270101)
XLA Ops:
  0.6 3.2 copy.49
  3.9 15.8 %all-to-all-start = ((f32[3,2,384,128]{3,0,1,2:T(4,128)}), f32[3,2,384,128]{3,0,1,2:T(4,128)S(1)}, u32[]{:S(2)}, u32[]{:S(2)}) async-start(f32[3,2,384,128]{3,0,1,2:T(4,128)} %copy.49), calls=%async_computation | async-start | bytes 3145728 | tf_op jit(solution)/shard_map/all_to_all | solution.py:73
  19.7 1.1 fusion.18
  20.8 38.9 %all-to-all-done = f32[3,2,384,128]{3,0,1,2:T(4,128)S(1)} async-done(((f32[3,2,384,128]{3,0,1,2:T(4,128)}), f32[3,2,384,128]{3,0,1,2:T(4,128)S(1)}, u32[]{:S(2)}, u32[]{:S(2)}) %all-to-all-start) | async-done | bytes 1179680 | tf_op jit(solution)/shard_map/all_to_all | solution.py:73
  61.5 1.1 fusion.7
  63.7 2.2 fusion.1
  65.9 10.8 copy.89
  76.7 19.5 %reshape.41 = f32[32,1,9216]{2,1,0:T(1,128)} reshape(f32[4096,3,2,12]{3,2,1,0:T(2,128)} %bitcast.62) | data formatting | bytes 2359296
  96.2 9.3 all-to-all-start.1
  106.2 1.1 fusion.6
  107.3 1.1 fusion.4
  108.4 1.1 fusion.3
  109.6 9.0 copy.90
  118.6 19.5 %reshape.43 = f32[32,1,9216]{2,1,0:T(1,128)} reshape(f32[4096,3,2,12]{3,2,1,0:T(2,128)} %bitcast.63) | data formatting | bytes 2359296
  138.1 12.9 all-to-all-start.2
  152.6 4.8 reduce.3
  157.4 21.8 %reshape.42 = f32[4096,3,2,12]{3,2,1,0:T(2,128)} reshape(f32[32,9216]{1,0:T(8,128)S(1)} %reduce.3) | data formatting | bytes 2359296
  179.2 10.2 copy.82
  190.7 1319.5 %all-gather.1 = f32[512,3,2]{1,2,0:T(2,128)S(1)} all-gather(f32[1,3,2]{1,2,0:T(2,128)S(1)} %bitcast.75), channel_id=2, replica_groups=mesh['gx'=32,'gz'=16] {'gx','gz'}, dimensions={0}, use_global_device_ids=true | all-gather | bytes 12312 | tf_op jit(solution)/shard_map/all_gather | solution.py:14
  1511.3 3.5 reduce.2
  1514.8 21.8 %reshape.44 = f32[4096,3,2,12]{3,2,1,0:T(2,128)} reshape(f32[32,9216]{1,0:T(8,128)S(1)} %reduce.2) | data formatting | bytes 2359296
  1536.7 10.2 copy.88
  1548.6 1.1 copy.68
  1549.7 1.1 copy.67
  (38 shorter events, 9.1 us)
Async XLA Ops:
  0.6 150.7 %copy-start = (f32[64]{0:T(128)S(1)}, f32[64]{0:T(128)}, u32[]{:S(2)}) copy-start(f32[64]{0:T(128)} %param.6) | copy-start | bytes 772
  3.9 55.9 %all-to-all-start = ((f32[3,2,384,128]{3,0,1,2:T(4,128)}), f32[3,2,384,128]{3,0,1,2:T(4,128)S(1)}, u32[]{:S(2)}, u32[]{:S(2)}) async-start(f32[3,2,384,128]{3,0,1,2:T(4,128)} %copy.49), calls=%async_computation | async-start | bytes 3145728 | tf_op jit(solution)/shard_map/all_to_all | solution.py:73
  60.5 0.6 copy-start.5
  60.5 2.0 copy-start.3
  60.5 0.9 copy-start.2
  96.2 42.0 %all-to-all-start.1 = ((f32[32,1,9216]{2,1,0:T(1,128)}), f32[32,1,9216]{2,1,0:T(1,128)}, u32[]{:S(2)}, u32[]{:S(2)}) async-start(f32[32,1,9216]{2,1,0:T(1,128)} %reshape.41), calls=%async_computation.1 | async-start | bytes 2359296 | tf_op jit(solution)/shard_map/all_to_all | solution.py:75
  105.5 0.8 copy-start.6
  106.2 1.1 copy-start.4
  138.1 13.0 copy-start.8
  138.1 13.0 copy-start.9
  138.1 1373.2 %all-to-all-start.2 = ((f32[32,1,9216]{2,1,0:T(1,128)}), f32[32,1,9216]{2,1,0:T(1,128)S(1)}, u32[]{:S(2)}, u32[]{:S(2)}) async-start(f32[32,1,9216]{2,1,0:T(1,128)} %reshape.43), calls=%async_computation.2 | async-start | bytes 2359296 | tf_op jit(solution)/shard_map/all_to_all | solution.py:76
  1546.8 0.9 copy-start.7
  1549.7 1.1 copy-start.1
